TPU v7x, 128 devices: a whole 4x4x4 slice. The times are simulated.
128 devices in a mesh: gx: 8 (over y, core), gy: 16 (over z, x).
Axes of the slice: x: 4, y: 4, z: 4, core: 2. Of those that a mesh axis runs over, the one named last changes fastest.
Arguments:
- right_side: float32 [256, 512, 256], P('gx', 'gy'), may hold values from -32 to 32
- phase: int32 [256, 512, 256], P('gx', 'gy'), may hold values from 1 to 3
- table: float32 [4], replicated, may hold values from 0.3 to 3
Outputs:
- solution_field: float32 [256, 512, 256], P('gx', 'gy')
- residual: float32 [256, 512, 256], P('gx', 'gy')
- pre_residual: float32 [256, 512, 256], P('gx', 'gy')
- residual_image: float32 [256, 512, 256], P('gx', 'gy')
Inputs may be any that keep to these rules, and one draw needn't show every extreme that they name: `phase`: labels 1 slag, 2 steel, 3 argon plume; label 0 stands for the lining outside the grid.
All inputs are finite; a program needn't handle non-finite values.
Results may differ from a plain program's by a relative error of at most 0.0003.
Values sent between devices are 32-bit elements; how exact they have to be, the bound alone decides.
No kernel may reach another device: no remote copies, remote signals or barrier semaphores. Data moves between devices by JAX's collectives and lax.ppermute only.
A program may use at most 64 MiB of HBM per device.

v0:
```python
import jax
import jax.numpy as jnp
from jax import lax
from jax.sharding import PartitionSpec as P

ITERS = 2
centre_value = 1.1
half_width = 0.9
ratio_sigma = centre_value / half_width
rho_first = 1.0 / ratio_sigma
rho_second = 1.0 / (2.0 * ratio_sigma - rho_first)
rho_third = 1.0 / (2.0 * ratio_sigma - rho_second)
start_scale = 1.0 / centre_value
keep_first = rho_second * rho_first
push_first = 2.0 * rho_second / half_width
keep_second = rho_third * rho_second
push_second = 2.0 * rho_third / half_width


def extended(block, sides, width):
    for axis, dim in sides:
        count = lax.axis_size(axis)
        forward = [(i, i + 1) for i in range(count - 1)]
        backward = [(target, source) for source, target in forward]
        low = lax.ppermute(
            lax.slice_in_dim(block, block.shape[dim] - width, None, axis=dim), axis, forward
        )
        high = lax.ppermute(lax.slice_in_dim(block, 0, width, axis=dim), axis, backward)
        block = jnp.concatenate([low, block, high], axis=dim)
    return block


def harmonic(left, right):
    return 2.0 * left * right / (left + right)


def coupling_set(sigma_padded):
    centre = sigma_padded[1:-1, 1:-1, 1:-1]
    to_west = harmonic(centre, sigma_padded[:-2, 1:-1, 1:-1])
    to_east = harmonic(centre, sigma_padded[2:, 1:-1, 1:-1])
    to_south = harmonic(centre, sigma_padded[1:-1, :-2, 1:-1])
    to_north = harmonic(centre, sigma_padded[1:-1, 2:, 1:-1])
    to_down = harmonic(centre, sigma_padded[1:-1, 1:-1, :-2])
    to_up = harmonic(centre, sigma_padded[1:-1, 1:-1, 2:])
    diagonal = to_west + to_east + to_south + to_north + to_down + to_up
    return (to_west, to_east, to_south, to_north, to_down, to_up, diagonal)


def lookup(labels, table):
    return jnp.where(
        labels == 1,
        table[1],
        jnp.where(labels == 2, table[2], jnp.where(labels == 3, table[3], table[0])),
    )


def operate_ext(padded_xy, couplings):
    to_west, to_east, to_south, to_north, to_down, to_up, diagonal = couplings
    padded_z = jnp.pad(padded_xy, ((0, 0), (0, 0), (1, 1)))
    centre = padded_xy[1:-1, 1:-1]
    beside = (
        to_west * padded_xy[:-2, 1:-1]
        + to_east * padded_xy[2:, 1:-1]
        + to_south * padded_xy[1:-1, :-2]
        + to_north * padded_xy[1:-1, 2:]
        + to_down * padded_z[1:-1, 1:-1, :-2]
        + to_up * padded_z[1:-1, 1:-1, 2:]
    )
    return diagonal * centre - beside


def local(right_side, phase, table):
    labels_ext = extended(phase, (("gx", 0), ("gy", 1)), 1)
    sigma_ext = lookup(jnp.pad(labels_ext, ((0, 0), (0, 0), (1, 1))), table)
    stored_set = coupling_set(sigma_ext)

    def composite(vector):
        set_zero = tuple((member for member in stored_set))
        diagonal = set_zero[6]

        def image_of(field):
            return operate_ext(extended(field, (("gx", 0), ("gy", 1)), 1), set_zero)

        first = start_scale * (vector / diagonal)
        change = keep_first * first + push_first * ((vector - image_of(first)) / diagonal)
        second = first + change
        change = keep_second * change + push_second * ((vector - image_of(second)) / diagonal)
        third = second + change
        return (third, image_of(third))

    solution_field = jnp.zeros_like(right_side)
    residual = right_side
    pre_residual, residual_image = composite(residual)
    image_dir = jnp.zeros_like(right_side)
    pre_dir = jnp.zeros_like(right_side)
    resid_dir = jnp.zeros_like(right_side)
    direction = jnp.zeros_like(right_side)
    energy_prev = jnp.float32(1.0)
    step_prev = jnp.float32(1.0)
    for iteration in range(ITERS):
        energy_now, curvature = lax.psum(
            (jnp.sum(residual * pre_residual), jnp.sum(residual_image * pre_residual)), ("gx", "gy")
        )
        pre_image, double_image = composite(residual_image)
        if iteration == 0:
            step_size = energy_now / curvature
            image_dir = double_image
            pre_dir = pre_image
            resid_dir = residual_image
            direction = pre_residual
        else:
            momentum = energy_now / energy_prev
            step_size = energy_now / (curvature - momentum * energy_now / step_prev)
            image_dir = double_image + momentum * image_dir
            pre_dir = pre_image + momentum * pre_dir
            resid_dir = residual_image + momentum * resid_dir
            direction = pre_residual + momentum * direction
        solution_field = solution_field + step_size * direction
        residual = residual - step_size * resid_dir
        pre_residual = pre_residual - step_size * pre_dir
        residual_image = residual_image - step_size * image_dir
        energy_prev = energy_now
        step_prev = step_size
    return (solution_field, residual, pre_residual, residual_image)


def solution(mesh):
    placed = (P("gx", "gy", None), P("gx", "gy", None), P())
    return jax.shard_map(
        local,
        mesh=mesh,
        in_specs=placed,
        out_specs=(
            P("gx", "gy", None),
            P("gx", "gy", None),
            P("gx", "gy", None),
            P("gx", "gy", None),
        ),
        check_vma=False,
    )
```

profile of v0, /device:TPU:39, one launch (start us, length us, event | category | flops | bytes accessed | tf_op | source)
XLA Modules:
  0.0 359.8 jit_solution(430377248482108931)
XLA Ops:
  1.4 3.8 %collective-permute-start = (s32[1,32,256]{2,1,0:T(8,128)S(1)}, s32[1,32,256]{2,1,0:T(8,128)S(1)}, u32[]{:S(2)}, u32[]{:S(2)}) collective-permute-start(s32[1,32,256]{2,1,0:T(8,128)S(1)} %get-tuple-element.70), channel_id=1, source_target_pairs={{0,16},{16,32},{32,48},{48,64},{64,80},{80,96},{96,112},{1,17},{17... | collective-permute-start | bytes 98312 | tf_op jit(solution)/shard_map/ppermute | solution.py:25
  10.5 3.5 collective-permute-start.2
  16.5 4.3 %collective-permute-done.3 = s32[34,1,256]{2,1,0:T(1,128)S(1)} collective-permute-done((s32[34,1,256]{2,1,0:T(1,128)S(1)}, s32[34,1,256]{2,1,0:T(1,128)S(1)}, u32[]{:S(2)}, u32[]{:S(2)}) %collective-permute-start.3) | collective-permute-done | bytes 34848 | tf_op jit(solution)/shard_map/ppermute | solution.py:28
  37.1 3.4 collective-permute-start.7
  40.5 3.4 collective-permute-done.7
  57.8 3.4 collective-permute-start.11
  61.2 3.4 collective-permute-done.11
  78.6 3.4 collective-permute-start.15
  82.0 3.4 collective-permute-done.15
  100.8 3.5 collective-permute-start.19
  121.5 3.4 collective-permute-start.23
  124.9 3.4 collective-permute-done.23
  142.3 3.4 collective-permute-start.27
  145.7 63.7 %all-reduce.11 = (f32[]{:T(128)}, f32[]{:T(128)}) all-reduce(f32[]{:T(128)} %get-tuple-element.7, f32[]{:T(128)} %get-tuple-element.6), channel_id=1, replica_groups=mesh['gx'=8,'gy'=16] {'gx','gy'}, use_global_device_ids=true, to_apply=%region_1.2 | all-reduce | flops 2 | bytes 16 | tf_op jit(solution)/shard_map/psum | solution.py:101
  213.0 6.4 %fusion.125 = (f32[32,32,256]{2,1,0:T(8,128)S(1)}, f32[32,32,256]{2,1,0:T(8,128)S(1)}, f32[32,32,256]{2,1,0:T(8,128)}) fusion(f32[32,32,256]{2,1,0:T(8,128)S(1)} %copy-done.7, f32[32,32,256]{2,1,0:T(8,128)S(1)} %copy-done.4, f32[32,32,256]{2,1,0:T(8,128)S(1)} %copy-done.1, f32[32,32,256]{2,1,0:T(8,128)S(1)} %get-tuple-element.27, ...), kind=kLoop, calls=%fused_computation.275 | loop fusion | flops 7864320 | bytes 13766660 | tf_op jit(solution)/shard_map/mul | solution.py:84
  219.5 4.5 %collective-permute-start.28 = (f32[1,32,256]{2,1,0:T(8,128)S(1)}, f32[1,32,256]{2,1,0:T(8,128)S(1)}, u32[]{:S(2)}, u32[]{:S(2)}) collective-permute-start(f32[1,32,256]{2,1,0:T(8,128)S(1)} %get-tuple-element.55), channel_id=1, source_target_pairs={{0,16},{16,32},{32,48},{48,64},{64,80},{80,96},{96,112},{1,17},{17... | collective-permute-start | bytes 98312 | tf_op jit(solution)/shard_map/ppermute | solution.py:25
  229.3 3.3 collective-permute-start.30
  234.6 4.8 %collective-permute-done.31 = f32[34,1,256]{2,1,0:T(1,128)S(1)} collective-permute-done((f32[34,1,256]{2,1,0:T(1,128)S(1)}, f32[34,1,256]{2,1,0:T(1,128)S(1)}, u32[]{:S(2)}, u32[]{:S(2)}) %collective-permute-start.31) | collective-permute-done | bytes 34848 | tf_op jit(solution)/shard_map/ppermute | solution.py:28
  240.4 3.5 fusion.128
  254.5 3.6 collective-permute-start.35
  259.3 62.3 %all-reduce.10 = (f32[]{:T(128)}, f32[]{:T(128)}) all-reduce(f32[]{:T(128)} %get-tuple-element.5, f32[]{:T(128)} %get-tuple-element.4), channel_id=1, replica_groups=mesh['gx'=8,'gy'=16] {'gx','gy'}, use_global_device_ids=true, to_apply=%region_5.6 | all-reduce | flops 2 | bytes 16 | tf_op jit(solution)/shard_map/psum | solution.py:101
  328.5 7.3 %multiply_subtract_fusion = (f32[32,32,256]{2,1,0:T(8,128)}, f32[32,32,256]{2,1,0:T(8,128)S(1)}) fusion(f32[32,32,256]{2,1,0:T(8,128)} %copy-done.9, f32[]{:T(128)S(6)} %div.70, f32[]{:T(128)S(6)} %div.72, f32[32,32,256]{2,1,0:T(8,128)} %copy-done.12, f32[]{:T(128)S(6)} %div.66, f32[32,32,256]{2,1,0:T(8,128)} %copy-done.23, f32[32,32,256]{2,1,0:T(8,128)} %copy-done.18, ...), kind=kLoop, calls=%fused_computation.254 | loop fusion | flops 9961472 | bytes 15863820 | tf_op jit(solution)/shard_map/sub | solution.py:120
  335.7 4.2 %collective-permute-start.36 = (f32[1,32,256]{2,1,0:T(8,128)S(1)}, f32[1,32,256]{2,1,0:T(8,128)S(1)}, u32[]{:S(2)}, u32[]{:S(2)}) collective-permute-start(f32[1,32,256]{2,1,0:T(8,128)S(1)} %get-tuple-element.51), channel_id=1, source_target_pairs={{0,16},{16,32},{32,48},{48,64},{64,80},{80,96},{96,112},{1,17},{17... | collective-permute-start | bytes 98312 | tf_op jit(solution)/shard_map/ppermute | solution.py:25
  356.3 3.5 fusion.5
  (158 shorter events, 139.8 us)
Async XLA Ops:
  1.4 5.7 %collective-permute-start = (s32[1,32,256]{2,1,0:T(8,128)S(1)}, s32[1,32,256]{2,1,0:T(8,128)S(1)}, u32[]{:S(2)}, u32[]{:S(2)}) collective-permute-start(s32[1,32,256]{2,1,0:T(8,128)S(1)} %get-tuple-element.70), channel_id=1, source_target_pairs={{0,16},{16,32},{32,48},{48,64},{64,80},{80,96},{96,112},{1,17},{17... | collective-permute-start | bytes 98312 | tf_op jit(solution)/shard_map/ppermute | solution.py:25
  10.5 6.0 %collective-permute-start.2 = (s32[34,1,256]{2,1,0:T(1,128)S(1)}, s32[34,1,256]{2,1,0:T(1,128)S(1)}, u32[]{:S(2)}, u32[]{:S(2)}) collective-permute-start(s32[34,1,256]{2,1,0:T(1,128)S(1)} %get-tuple-element.49), channel_id=1, source_target_pairs={{0,1},{1,2},{2,3},{3,4},{4,5},{5,6},{6,7},{7,8},{8,9},{9,10},{10,1... | collective-permute-start | bytes 104456 | tf_op jit(solution)/shard_map/ppermute | solution.py:25
  13.9 6.8 %collective-permute-start.3 = (s32[34,1,256]{2,1,0:T(1,128)S(1)}, s32[34,1,256]{2,1,0:T(1,128)S(1)}, u32[]{:S(2)}, u32[]{:S(2)}) collective-permute-start(s32[34,1,256]{2,1,0:T(1,128)S(1)} %get-tuple-element.50), channel_id=1, source_target_pairs={{1,0},{2,1},{3,2},{4,3},{5,4},{6,5},{7,6},{8,7},{9,8},{10,9},{11,1... | collective-permute-start | bytes 104456 | tf_op jit(solution)/shard_map/ppermute | solution.py:28
  26.5 5.3 %collective-permute-start.4 = (f32[1,32,256]{2,1,0:T(8,128)S(1)}, f32[1,32,256]{2,1,0:T(8,128)S(1)}, u32[]{:S(2)}, u32[]{:S(2)}) collective-permute-start(f32[1,32,256]{2,1,0:T(8,128)S(1)} %get-tuple-element.67), channel_id=1, source_target_pairs={{0,16},{16,32},{32,48},{48,64},{64,80},{80,96},{96,112},{1,17},{17... | collective-permute-start | bytes 98312 | tf_op jit(solution)/shard_map/ppermute | solution.py:25
  35.2 5.3 %collective-permute-start.6 = (f32[34,1,256]{2,1,0:T(1,128)S(1)}, f32[34,1,256]{2,1,0:T(1,128)S(1)}, u32[]{:S(2)}, u32[]{:S(2)}) collective-permute-start(f32[34,1,256]{2,1,0:T(1,128)S(1)} %get-tuple-element.47), channel_id=1, source_target_pairs={{0,1},{1,2},{2,3},{3,4},{4,5},{5,6},{6,7},{7,8},{8,9},{9,10},{10,1... | collective-permute-start | bytes 104456 | tf_op jit(solution)/shard_map/ppermute | solution.py:25
  37.1 6.8 %collective-permute-start.7 = (f32[34,1,256]{2,1,0:T(1,128)S(1)}, f32[34,1,256]{2,1,0:T(1,128)S(1)}, u32[]{:S(2)}, u32[]{:S(2)}) collective-permute-start(f32[34,1,256]{2,1,0:T(1,128)S(1)} %get-tuple-element.48), channel_id=1, source_target_pairs={{1,0},{2,1},{3,2},{4,3},{5,4},{6,5},{7,6},{8,7},{9,8},{10,9},{11,1... | collective-permute-start | bytes 104456 | tf_op jit(solution)/shard_map/ppermute | solution.py:28
  55.9 5.3 %collective-permute-start.10 = (f32[34,1,256]{2,1,0:T(1,128)S(1)}, f32[34,1,256]{2,1,0:T(1,128)S(1)}, u32[]{:S(2)}, u32[]{:S(2)}) collective-permute-start(f32[34,1,256]{2,1,0:T(1,128)S(1)} %get-tuple-element.45), channel_id=1, source_target_pairs={{0,1},{1,2},{2,3},{3,4},{4,5},{5,6},{6,7},{7,8},{8,9},{9,10},{10,1... | collective-permute-start | bytes 104456 | tf_op jit(solution)/shard_map/ppermute | solution.py:25
  57.8 6.8 %collective-permute-start.11 = (f32[34,1,256]{2,1,0:T(1,128)S(1)}, f32[34,1,256]{2,1,0:T(1,128)S(1)}, u32[]{:S(2)}, u32[]{:S(2)}) collective-permute-start(f32[34,1,256]{2,1,0:T(1,128)S(1)} %get-tuple-element.46), channel_id=1, source_target_pairs={{1,0},{2,1},{3,2},{4,3},{5,4},{6,5},{7,6},{8,7},{9,8},{10,9},{11,1... | collective-permute-start | bytes 104456 | tf_op jit(solution)/shard_map/ppermute | solution.py:28
  76.7 5.3 %collective-permute-start.14 = (f32[34,1,256]{2,1,0:T(1,128)S(1)}, f32[34,1,256]{2,1,0:T(1,128)S(1)}, u32[]{:S(2)}, u32[]{:S(2)}) collective-permute-start(f32[34,1,256]{2,1,0:T(1,128)S(1)} %get-tuple-element.43), channel_id=1, source_target_pairs={{0,1},{1,2},{2,3},{3,4},{4,5},{5,6},{6,7},{7,8},{8,9},{9,10},{10,1... | collective-permute-start | bytes 104456 | tf_op jit(solution)/shard_map/ppermute | solution.py:25
  78.6 6.8 %collective-permute-start.15 = (f32[34,1,256]{2,1,0:T(1,128)S(1)}, f32[34,1,256]{2,1,0:T(1,128)S(1)}, u32[]{:S(2)}, u32[]{:S(2)}) collective-permute-start(f32[34,1,256]{2,1,0:T(1,128)S(1)} %get-tuple-element.44), channel_id=1, source_target_pairs={{1,0},{2,1},{3,2},{4,3},{5,4},{6,5},{7,6},{8,7},{9,8},{10,9},{11,1... | collective-permute-start | bytes 104456 | tf_op jit(solution)/shard_map/ppermute | solution.py:28
  98.8 5.5 %collective-permute-start.18 = (f32[34,1,256]{2,1,0:T(1,128)S(1)}, f32[34,1,256]{2,1,0:T(1,128)S(1)}, u32[]{:S(2)}, u32[]{:S(2)}) collective-permute-start(f32[34,1,256]{2,1,0:T(1,128)S(1)} %get-tuple-element.41), channel_id=1, source_target_pairs={{0,1},{1,2},{2,3},{3,4},{4,5},{5,6},{6,7},{7,8},{8,9},{9,10},{10,1... | collective-permute-start | bytes 104456 | tf_op jit(solution)/shard_map/ppermute | solution.py:25
  100.8 6.8 %collective-permute-start.19 = (f32[34,1,256]{2,1,0:T(1,128)S(1)}, f32[34,1,256]{2,1,0:T(1,128)S(1)}, u32[]{:S(2)}, u32[]{:S(2)}) collective-permute-start(f32[34,1,256]{2,1,0:T(1,128)S(1)} %get-tuple-element.42), channel_id=1, source_target_pairs={{1,0},{2,1},{3,2},{4,3},{5,4},{6,5},{7,6},{8,7},{9,8},{10,9},{11,1... | collective-permute-start | bytes 104456 | tf_op jit(solution)/shard_map/ppermute | solution.py:28
  119.6 5.3 %collective-permute-start.22 = (f32[34,1,256]{2,1,0:T(1,128)S(1)}, f32[34,1,256]{2,1,0:T(1,128)S(1)}, u32[]{:S(2)}, u32[]{:S(2)}) collective-permute-start(f32[34,1,256]{2,1,0:T(1,128)S(1)} %get-tuple-element.39), channel_id=1, source_target_pairs={{0,1},{1,2},{2,3},{3,4},{4,5},{5,6},{6,7},{7,8},{8,9},{9,10},{10,1... | collective-permute-start | bytes 104456 | tf_op jit(solution)/shard_map/ppermute | solution.py:25
  121.5 6.8 %collective-permute-start.23 = (f32[34,1,256]{2,1,0:T(1,128)S(1)}, f32[34,1,256]{2,1,0:T(1,128)S(1)}, u32[]{:S(2)}, u32[]{:S(2)}) collective-permute-start(f32[34,1,256]{2,1,0:T(1,128)S(1)} %get-tuple-element.40), channel_id=1, source_target_pairs={{1,0},{2,1},{3,2},{4,3},{5,4},{6,5},{7,6},{8,7},{9,8},{10,9},{11,1... | collective-permute-start | bytes 104456 | tf_op jit(solution)/shard_map/ppermute | solution.py:28
  140.4 70.3 %collective-permute-start.26 = (f32[34,1,256]{2,1,0:T(1,128)S(1)}, f32[34,1,256]{2,1,0:T(1,128)S(1)}, u32[]{:S(2)}, u32[]{:S(2)}) collective-permute-start(f32[34,1,256]{2,1,0:T(1,128)S(1)} %get-tuple-element.37), channel_id=1, source_target_pairs={{0,1},{1,2},{2,3},{3,4},{4,5},{5,6},{6,7},{7,8},{8,9},{9,10},{10,1... | collective-permute-start | bytes 104456 | tf_op jit(solution)/shard_map/ppermute | solution.py:25
  142.3 68.4 %collective-permute-start.27 = (f32[34,1,256]{2,1,0:T(1,128)S(1)}, f32[34,1,256]{2,1,0:T(1,128)S(1)}, u32[]{:S(2)}, u32[]{:S(2)}) collective-permute-start(f32[34,1,256]{2,1,0:T(1,128)S(1)} %get-tuple-element.38), channel_id=1, source_target_pairs={{1,0},{2,1},{3,2},{4,3},{5,4},{6,5},{7,6},{8,7},{9,8},{10,9},{11,1... | collective-permute-start | bytes 104456 | tf_op jit(solution)/shard_map/ppermute | solution.py:28
  219.5 6.4 %collective-permute-start.28 = (f32[1,32,256]{2,1,0:T(8,128)S(1)}, f32[1,32,256]{2,1,0:T(8,128)S(1)}, u32[]{:S(2)}, u32[]{:S(2)}) collective-permute-start(f32[1,32,256]{2,1,0:T(8,128)S(1)} %get-tuple-element.55), channel_id=1, source_target_pairs={{0,16},{16,32},{32,48},{48,64},{64,80},{80,96},{96,112},{1,17},{17... | collective-permute-start | bytes 98312 | tf_op jit(solution)/shard_map/ppermute | solution.py:25
  229.3 5.3 %collective-permute-start.30 = (f32[34,1,256]{2,1,0:T(1,128)S(1)}, f32[34,1,256]{2,1,0:T(1,128)S(1)}, u32[]{:S(2)}, u32[]{:S(2)}) collective-permute-start(f32[34,1,256]{2,1,0:T(1,128)S(1)} %get-tuple-element.35), channel_id=1, source_target_pairs={{0,1},{1,2},{2,3},{3,4},{4,5},{5,6},{6,7},{7,8},{8,9},{9,10},{10,1... | collective-permute-start | bytes 104456 | tf_op jit(solution)/shard_map/ppermute | solution.py:25
  232.6 6.8 %collective-permute-start.31 = (f32[34,1,256]{2,1,0:T(1,128)S(1)}, f32[34,1,256]{2,1,0:T(1,128)S(1)}, u32[]{:S(2)}, u32[]{:S(2)}) collective-permute-start(f32[34,1,256]{2,1,0:T(1,128)S(1)} %get-tuple-element.36), channel_id=1, source_target_pairs={{1,0},{2,1},{3,2},{4,3},{5,4},{6,5},{7,6},{8,7},{9,8},{10,9},{11,1... | collective-permute-start | bytes 104456 | tf_op jit(solution)/shard_map/ppermute | solution.py:28
  252.6 73.5 %collective-permute-start.34 = (f32[34,1,256]{2,1,0:T(1,128)S(1)}, f32[34,1,256]{2,1,0:T(1,128)S(1)}, u32[]{:S(2)}, u32[]{:S(2)}) collective-permute-start(f32[34,1,256]{2,1,0:T(1,128)S(1)} %get-tuple-element.33), channel_id=1, source_target_pairs={{0,1},{1,2},{2,3},{3,4},{4,5},{5,6},{6,7},{7,8},{8,9},{9,10},{10,1... | collective-permute-start | bytes 104456 | tf_op jit(solution)/shard_map/ppermute | solution.py:25
  254.5 71.6 %collective-permute-start.35 = (f32[34,1,256]{2,1,0:T(1,128)S(1)}, f32[34,1,256]{2,1,0:T(1,128)S(1)}, u32[]{:S(2)}, u32[]{:S(2)}) collective-permute-start(f32[34,1,256]{2,1,0:T(1,128)S(1)} %get-tuple-element.34), channel_id=1, source_target_pairs={{1,0},{2,1},{3,2},{4,3},{5,4},{6,5},{7,6},{8,7},{9,8},{10,9},{11,1... | collective-permute-start | bytes 104456 | tf_op jit(solution)/shard_map/ppermute | solution.py:28
  335.7 6.1 %collective-permute-start.36 = (f32[1,32,256]{2,1,0:T(8,128)S(1)}, f32[1,32,256]{2,1,0:T(8,128)S(1)}, u32[]{:S(2)}, u32[]{:S(2)}) collective-permute-start(f32[1,32,256]{2,1,0:T(8,128)S(1)} %get-tuple-element.51), channel_id=1, source_target_pairs={{0,16},{16,32},{32,48},{48,64},{64,80},{80,96},{96,112},{1,17},{17... | collective-permute-start | bytes 98312 | tf_op jit(solution)/shard_map/ppermute | solution.py:25
  345.2 7.3 %collective-permute-start.38 = (f32[34,1,256]{2,1,0:T(1,128)S(1)}, f32[34,1,256]{2,1,0:T(1,128)S(1)}, u32[]{:S(2)}, u32[]{:S(2)}) collective-permute-start(f32[34,1,256]{2,1,0:T(1,128)S(1)} %get-tuple-element.31), channel_id=1, source_target_pairs={{0,1},{1,2},{2,3},{3,4},{4,5},{5,6},{6,7},{7,8},{8,9},{9,10},{10,1... | collective-permute-start | bytes 104456 | tf_op jit(solution)/shard_map/ppermute | solution.py:25
  348.5 6.8 %collective-permute-start.39 = (f32[34,1,256]{2,1,0:T(1,128)S(1)}, f32[34,1,256]{2,1,0:T(1,128)S(1)}, u32[]{:S(2)}, u32[]{:S(2)}) collective-permute-start(f32[34,1,256]{2,1,0:T(1,128)S(1)} %get-tuple-element.32), channel_id=1, source_target_pairs={{1,0},{2,1},{3,2},{4,3},{5,4},{6,5},{7,6},{8,7},{9,8},{10,9},{11,1... | collective-permute-start | bytes 104456 | tf_op jit(solution)/shard_map/ppermute | solution.py:28
  (42 other events, 728.7 us)
where the time goes:
time: 361 us; the launch traced here: 360 us
  blocking collectives  126 us (35%)
  starting transfers between devices  107 us (30%)
  waiting for transfers between devices  60.4 us (17%)
  other arithmetic  56.1 us (16%)
  between operations  7.42 us (2%)
    psum x2, blocking collectives, local(): lax.psum((jnp.sum(residual * pre_residual), jnp.sum(residual_image * pre_...  126 us
    ppermute x20, waiting for transfers between devices, extended(): lax.ppermute(lax.slice_in_dim(block, 0, width, axis=dim), axis, backward)  60.4 us
    ppermute x20, starting transfers between devices, extended(): lax.ppermute(lax.slice_in_dim(block, block.shape[dim] - width, None, axis...  57.9 us
    ppermute x20, starting transfers between devices, extended(): lax.ppermute(lax.slice_in_dim(block, 0, width, axis=dim), axis, backward)  49 us
    concatenate x10, other arithmetic, extended(): block = jnp.concatenate([low, block, high], axis=dim)  11.3 us
    mul x3, other arithmetic, composite(): first = start_scale * (vector / diagonal)  9.5 us
    add x3, other arithmetic, composite(): second = first + change  8.92 us
    sub x1, other arithmetic, local(): pre_residual = pre_residual - step_size * pre_dir  7.26 us
  transfers between devices with their start and end apart: 40, of which 18 were waited for; matrix products, arithmetic and copies ran while one was open for 1% of the time, Pallas kernels for 0%

commit v1 on v0

--- a/solution.py
+++ b/solution.py
@@ -99,7 +99,10 @@
     step_prev = jnp.float32(1.0)
     for iteration in range(ITERS):
         energy_now, curvature = lax.psum(
-            (jnp.sum(residual * pre_residual), jnp.sum(residual_image * pre_residual)), ("gx", "gy")
+            lax.psum(
+                (jnp.sum(residual * pre_residual), jnp.sum(residual_image * pre_residual)), "gx"
+            ),
+            "gy",
         )
         pre_image, double_image = composite(residual_image)
         if iteration == 0:

time: 361 us -> 325 us (0.900)
  blocking collectives: 126 us -> 71.7 us
  starting transfers between devices: 107 us -> 124 us
    psum x2, blocking collectives: 126 us -> 22.8 us  [local(): lax.psum((jnp.sum(residual * pre_residual), jnp.sum(residual_image * pre_...]
    psum x0 -> x2, blocking collectives: none -> 49 us  [local(): lax.psum(lax.psum((jnp.sum(residual * pre_residual), jnp.sum(residual_ima...]
    ppermute x20, starting transfers between devices: 57.9 us -> 75.3 us  [extended(): lax.ppermute(lax.slice_in_dim(block, block.shape[dim] - width, None, axis...]
  transfers between devices with their start and end apart: 40 -> 40, of which waited for: 18 -> 18; matrix products, arithmetic and copies ran while one was open for 1% -> 2% of each run, Pallas kernels for 0% -> 0%
where the time goes in v1:
time: 325 us; the launch traced here: 323 us
  starting transfers between devices  124 us (38%)
  blocking collectives  71.7 us (22%)
  waiting for transfers between devices  60.1 us (18%)
  other arithmetic  56.4 us (17%)
  between operations  7.72 us (2%)
    ppermute x20, starting transfers between devices, extended(): lax.ppermute(lax.slice_in_dim(block, block.shape[dim] - width, None, axis...  75.3 us
    ppermute x20, waiting for transfers between devices, extended(): lax.ppermute(lax.slice_in_dim(block, 0, width, axis=dim), axis, backward)  60.1 us
    ppermute x20, starting transfers between devices, extended(): lax.ppermute(lax.slice_in_dim(block, 0, width, axis=dim), axis, backward)  49.1 us
    psum x2, blocking collectives, local(): lax.psum(lax.psum((jnp.sum(residual * pre_residual), jnp.sum(residual_ima...  49 us
    psum x2, blocking collectives, local(): lax.psum((jnp.sum(residual * pre_residual), jnp.sum(residual_image * pre_...  22.8 us
    concatenate x10, other arithmetic, extended(): block = jnp.concatenate([low, block, high], axis=dim)  11.3 us
    mul x3, other arithmetic, composite(): first = start_scale * (vector / diagonal)  9.67 us
    add x3, other arithmetic, composite(): second = first + change  8.9 us
  transfers between devices with their start and end apart: 40, of which 18 were waited for; matrix products, arithmetic and copies ran while one was open for 2% of the time, Pallas kernels for 0%

profile of v1, /device:TPU:39, one launch (start us, length us, event | category | flops | bytes accessed | tf_op | source)
XLA Modules:
  0.0 323.3 jit_solution(4925745602213888747)
XLA Ops:
  1.4 3.8 %collective-permute-start = (s32[1,32,256]{2,1,0:T(8,128)S(1)}, s32[1,32,256]{2,1,0:T(8,128)S(1)}, u32[]{:S(2)}, u32[]{:S(2)}) collective-permute-start(s32[1,32,256]{2,1,0:T(8,128)S(1)} %get-tuple-element.74), channel_id=1, source_target_pairs={{0,16},{16,32},{32,48},{48,64},{64,80},{80,96},{96,112},{1,17},{17... | collective-permute-start | bytes 98312 | tf_op jit(solution)/shard_map/ppermute | solution.py:25
  10.5 3.5 %collective-permute-start.2 = (s32[34,1,256]{2,1,0:T(1,128)S(1)}, s32[34,1,256]{2,1,0:T(1,128)S(1)}, u32[]{:S(2)}, u32[]{:S(2)}) collective-permute-start(s32[34,1,256]{2,1,0:T(1,128)S(1)} %get-tuple-element.53), channel_id=1, source_target_pairs={{0,1},{1,2},{2,3},{3,4},{4,5},{5,6},{6,7},{7,8},{8,9},{9,10},{10,1... | collective-permute-start | bytes 104456 | tf_op jit(solution)/shard_map/ppermute | solution.py:25
  16.5 4.3 %collective-permute-done.3 = s32[34,1,256]{2,1,0:T(1,128)S(1)} collective-permute-done((s32[34,1,256]{2,1,0:T(1,128)S(1)}, s32[34,1,256]{2,1,0:T(1,128)S(1)}, u32[]{:S(2)}, u32[]{:S(2)}) %collective-permute-start.3) | collective-permute-done | bytes 34848 | tf_op jit(solution)/shard_map/ppermute | solution.py:28
  40.5 3.4 %collective-permute-done.7 = f32[34,1,256]{2,1,0:T(1,128)S(1)} collective-permute-done((f32[34,1,256]{2,1,0:T(1,128)S(1)}, f32[34,1,256]{2,1,0:T(1,128)S(1)}, u32[]{:S(2)}, u32[]{:S(2)}) %collective-permute-start.7) | collective-permute-done | bytes 34848 | tf_op jit(solution)/shard_map/ppermute | solution.py:28
  57.8 3.4 %collective-permute-start.11 = (f32[34,1,256]{2,1,0:T(1,128)S(1)}, f32[34,1,256]{2,1,0:T(1,128)S(1)}, u32[]{:S(2)}, u32[]{:S(2)}) collective-permute-start(f32[34,1,256]{2,1,0:T(1,128)S(1)} %get-tuple-element.50), channel_id=1, source_target_pairs={{1,0},{2,1},{3,2},{4,3},{5,4},{6,5},{7,6},{8,7},{9,8},{10,9},{11,1... | collective-permute-start | bytes 104456 | tf_op jit(solution)/shard_map/ppermute | solution.py:28
  61.2 3.4 %collective-permute-done.11 = f32[34,1,256]{2,1,0:T(1,128)S(1)} collective-permute-done((f32[34,1,256]{2,1,0:T(1,128)S(1)}, f32[34,1,256]{2,1,0:T(1,128)S(1)}, u32[]{:S(2)}, u32[]{:S(2)}) %collective-permute-start.11) | collective-permute-done | bytes 34848 | tf_op jit(solution)/shard_map/ppermute | solution.py:28
  82.0 3.4 %collective-permute-done.15 = f32[34,1,256]{2,1,0:T(1,128)S(1)} collective-permute-done((f32[34,1,256]{2,1,0:T(1,128)S(1)}, f32[34,1,256]{2,1,0:T(1,128)S(1)}, u32[]{:S(2)}, u32[]{:S(2)}) %collective-permute-start.15) | collective-permute-done | bytes 34848 | tf_op jit(solution)/shard_map/ppermute | solution.py:28
  100.7 3.5 %collective-permute-start.19 = (f32[34,1,256]{2,1,0:T(1,128)S(1)}, f32[34,1,256]{2,1,0:T(1,128)S(1)}, u32[]{:S(2)}, u32[]{:S(2)}) collective-permute-start(f32[34,1,256]{2,1,0:T(1,128)S(1)} %get-tuple-element.46), channel_id=1, source_target_pairs={{1,0},{2,1},{3,2},{4,3},{5,4},{6,5},{7,6},{8,7},{9,8},{10,9},{11,1... | collective-permute-start | bytes 104456 | tf_op jit(solution)/shard_map/ppermute | solution.py:28
  124.8 3.4 %collective-permute-done.23 = f32[34,1,256]{2,1,0:T(1,128)S(1)} collective-permute-done((f32[34,1,256]{2,1,0:T(1,128)S(1)}, f32[34,1,256]{2,1,0:T(1,128)S(1)}, u32[]{:S(2)}, u32[]{:S(2)}) %collective-permute-start.23) | collective-permute-done | bytes 34848 | tf_op jit(solution)/shard_map/ppermute | solution.py:28
  142.3 3.4 %collective-permute-start.27 = (f32[34,1,256]{2,1,0:T(1,128)S(1)}, f32[34,1,256]{2,1,0:T(1,128)S(1)}, u32[]{:S(2)}, u32[]{:S(2)}) collective-permute-start(f32[34,1,256]{2,1,0:T(1,128)S(1)} %get-tuple-element.42), channel_id=1, source_target_pairs={{1,0},{2,1},{3,2},{4,3},{5,4},{6,5},{7,6},{8,7},{9,8},{10,9},{11,1... | collective-permute-start | bytes 104456 | tf_op jit(solution)/shard_map/ppermute | solution.py:28
  145.7 11.9 %all-reduce.13 = (f32[]{:T(128)}, f32[]{:T(128)}) all-reduce(f32[]{:T(128)} %get-tuple-element.7, f32[]{:T(128)} %get-tuple-element.6), channel_id=1, replica_groups=mesh['gx'=8,'gy'=16] {'gx'}, use_global_device_ids=true, to_apply=%region_1.2 | all-reduce | flops 2 | bytes 16 | tf_op jit(solution)/shard_map/psum | solution.py:102
  157.5 24.4 %all-reduce.11 = (f32[]{:T(128)}, f32[]{:T(128)}) all-reduce(f32[]{:T(128)} %get-tuple-element.14, f32[]{:T(128)} %get-tuple-element.15), channel_id=1, replica_groups=mesh['gx'=8,'gy'=16] {'gy'}, use_global_device_ids=true, to_apply=%region_2.3 | all-reduce | flops 2 | bytes 16 | tf_op jit(solution)/shard_map/psum | solution.py:101
  185.7 6.6 %fusion.125 = (f32[32,32,256]{2,1,0:T(8,128)S(1)}, f32[32,32,256]{2,1,0:T(8,128)S(1)}, f32[32,32,256]{2,1,0:T(8,128)}) fusion(f32[32,32,256]{2,1,0:T(8,128)S(1)} %copy-done.7, f32[32,32,256]{2,1,0:T(8,128)S(1)} %copy-done.4, f32[32,32,256]{2,1,0:T(8,128)S(1)} %copy-done.1, f32[32,32,256]{2,1,0:T(8,128)S(1)} %get-tuple-element.31, ...), kind=kLoop, calls=%fused_computation.275 | loop fusion | flops 7864320 | bytes 13766660 | tf_op jit(solution)/shard_map/mul | solution.py:84
  192.3 10.5 %collective-permute-start.28 = (f32[1,32,256]{2,1,0:T(8,128)S(1)}, f32[1,32,256]{2,1,0:T(8,128)S(1)}, u32[]{:S(2)}, u32[]{:S(2)}) collective-permute-start(f32[1,32,256]{2,1,0:T(8,128)S(1)} %get-tuple-element.59), channel_id=1, source_target_pairs={{0,16},{16,32},{32,48},{48,64},{64,80},{80,96},{96,112},{1,17},{17... | collective-permute-start | bytes 98312 | tf_op jit(solution)/shard_map/ppermute | solution.py:25
  208.2 5.5 %collective-permute-start.30 = (f32[34,1,256]{2,1,0:T(1,128)S(1)}, f32[34,1,256]{2,1,0:T(1,128)S(1)}, u32[]{:S(2)}, u32[]{:S(2)}) collective-permute-start(f32[34,1,256]{2,1,0:T(1,128)S(1)} %get-tuple-element.39), channel_id=1, source_target_pairs={{0,1},{1,2},{2,3},{3,4},{4,5},{5,6},{6,7},{7,8},{8,9},{9,10},{10,1... | collective-permute-start | bytes 104456 | tf_op jit(solution)/shard_map/ppermute | solution.py:25
  215.6 4.9 %collective-permute-done.31 = f32[34,1,256]{2,1,0:T(1,128)S(1)} collective-permute-done((f32[34,1,256]{2,1,0:T(1,128)S(1)}, f32[34,1,256]{2,1,0:T(1,128)S(1)}, u32[]{:S(2)}, u32[]{:S(2)}) %collective-permute-start.31) | collective-permute-done | bytes 34848 | tf_op jit(solution)/shard_map/ppermute | solution.py:28
  221.4 3.5 %fusion.128 = (f32[32,32,256]{2,1,0:T(8,128)S(1)}, f32[32,32,256]{2,1,0:T(8,128)}) fusion(f32[32,32,256]{2,1,0:T(8,128)S(1)} %get-tuple-element.20, f32[32,32,256]{2,1,0:T(8,128)S(1)} %get-tuple-element.21, f32[32,32,256]{2,1,0:T(8,128)S(1)} %copy-done.7, f32[34,34,258]{2,1,0:T(8,128)S(1)} %select_maximum_fusion.8, f32[32,32,256]{2,1,0:T(8,128)S(1)} %copy-done.4, ...), kind=kLoop, calls=%fused_computation.307 | loop fusion | flops 8650752 | bytes 12718080 | tf_op jit(solution)/shard_map/add | solution.py:86
  224.9 3.5 %collective-permute-start.32 = (f32[1,32,256]{2,1,0:T(8,128)S(1)}, f32[1,32,256]{2,1,0:T(8,128)S(1)}, u32[]{:S(2)}, u32[]{:S(2)}) collective-permute-start(f32[1,32,256]{2,1,0:T(8,128)S(1)} %get-tuple-element.57), channel_id=1, source_target_pairs={{0,16},{16,32},{32,48},{48,64},{64,80},{80,96},{96,112},{1,17},{17... | collective-permute-start | bytes 98312 | tf_op jit(solution)/shard_map/ppermute | solution.py:25
  240.3 10.9 %all-reduce.12 = (f32[]{:T(128)}, f32[]{:T(128)}) all-reduce(f32[]{:T(128)} %get-tuple-element.5, f32[]{:T(128)} %get-tuple-element.4), channel_id=1, replica_groups=mesh['gx'=8,'gy'=16] {'gx'}, use_global_device_ids=true, to_apply=%region_7.8 | all-reduce | flops 2 | bytes 16 | tf_op jit(solution)/shard_map/psum | solution.py:102
  251.2 24.6 %all-reduce.10 = (f32[]{:T(128)}, f32[]{:T(128)}) all-reduce(f32[]{:T(128)} %get-tuple-element.12, f32[]{:T(128)} %get-tuple-element.13), channel_id=1, replica_groups=mesh['gx'=8,'gy'=16] {'gy'}, use_global_device_ids=true, to_apply=%region_8.9 | all-reduce | flops 2 | bytes 16 | tf_op jit(solution)/shard_map/psum | solution.py:101
  282.9 7.4 %multiply_subtract_fusion = (f32[32,32,256]{2,1,0:T(8,128)}, f32[32,32,256]{2,1,0:T(8,128)S(1)}) fusion(f32[32,32,256]{2,1,0:T(8,128)} %copy-done.9, f32[]{:T(128)S(6)} %div.70, f32[]{:T(128)S(6)} %div.72, f32[32,32,256]{2,1,0:T(8,128)} %copy-done.12, f32[]{:T(128)S(6)} %div.66, f32[32,32,256]{2,1,0:T(8,128)} %copy-done.23, f32[32,32,256]{2,1,0:T(8,128)} %copy-done.18, ...), kind=kLoop, calls=%fused_computation.254 | loop fusion | flops 9961472 | bytes 15863820 | tf_op jit(solution)/shard_map/sub | solution.py:123
  290.3 10.8 %collective-permute-start.36 = (f32[1,32,256]{2,1,0:T(8,128)S(1)}, f32[1,32,256]{2,1,0:T(8,128)S(1)}, u32[]{:S(2)}, u32[]{:S(2)}) collective-permute-start(f32[1,32,256]{2,1,0:T(8,128)S(1)} %get-tuple-element.55), channel_id=1, source_target_pairs={{0,16},{16,32},{32,48},{48,64},{64,80},{80,96},{96,112},{1,17},{17... | collective-permute-start | bytes 98312 | tf_op jit(solution)/shard_map/ppermute | solution.py:25
  306.4 5.6 %collective-permute-start.38 = (f32[34,1,256]{2,1,0:T(1,128)S(1)}, f32[34,1,256]{2,1,0:T(1,128)S(1)}, u32[]{:S(2)}, u32[]{:S(2)}) collective-permute-start(f32[34,1,256]{2,1,0:T(1,128)S(1)} %get-tuple-element.35), channel_id=1, source_target_pairs={{0,1},{1,2},{2,3},{3,4},{4,5},{5,6},{6,7},{7,8},{8,9},{9,10},{10,1... | collective-permute-start | bytes 104456 | tf_op jit(solution)/shard_map/ppermute | solution.py:25
  319.8 3.5 %fusion.5 = f32[32,32,256]{2,1,0:T(8,128)} fusion(f32[32,32,256]{2,1,0:T(8,128)S(1)} %copy-done.19, f32[32,32,256]{2,1,0:T(8,128)S(1)} %copy-done.8, f32[34,34,258]{2,1,0:T(8,128)S(1)} %select_maximum_fusion, f32[32,32,256]{2,1,0:T(8,128)S(1)} %copy-done.5, f32[32,32,256]{2,1,0:T(8,128)S(1)} %copy-done.2, f32[34,1,256]{2,1,0:T(1,128)S(1)} %collective-permute-done.39, ...), kind=kLoop, calls=%fused_computation.49 | loop fusion | flops 7864320 | bytes 12718088 | tf_op jit(solution)/shard_map/sub | solution.py:124
  (160 shorter events, 146.6 us)
Async XLA Ops:
  1.4 5.7 %collective-permute-start = (s32[1,32,256]{2,1,0:T(8,128)S(1)}, s32[1,32,256]{2,1,0:T(8,128)S(1)}, u32[]{:S(2)}, u32[]{:S(2)}) collective-permute-start(s32[1,32,256]{2,1,0:T(8,128)S(1)} %get-tuple-element.74), channel_id=1, source_target_pairs={{0,16},{16,32},{32,48},{48,64},{64,80},{80,96},{96,112},{1,17},{17... | collective-permute-start | bytes 98312 | tf_op jit(solution)/shard_map/ppermute | solution.py:25
  10.5 6.0 %collective-permute-start.2 = (s32[34,1,256]{2,1,0:T(1,128)S(1)}, s32[34,1,256]{2,1,0:T(1,128)S(1)}, u32[]{:S(2)}, u32[]{:S(2)}) collective-permute-start(s32[34,1,256]{2,1,0:T(1,128)S(1)} %get-tuple-element.53), channel_id=1, source_target_pairs={{0,1},{1,2},{2,3},{3,4},{4,5},{5,6},{6,7},{7,8},{8,9},{9,10},{10,1... | collective-permute-start | bytes 104456 | tf_op jit(solution)/shard_map/ppermute | solution.py:25
  13.9 6.8 %collective-permute-start.3 = (s32[34,1,256]{2,1,0:T(1,128)S(1)}, s32[34,1,256]{2,1,0:T(1,128)S(1)}, u32[]{:S(2)}, u32[]{:S(2)}) collective-permute-start(s32[34,1,256]{2,1,0:T(1,128)S(1)} %get-tuple-element.54), channel_id=1, source_target_pairs={{1,0},{2,1},{3,2},{4,3},{5,4},{6,5},{7,6},{8,7},{9,8},{10,9},{11,1... | collective-permute-start | bytes 104456 | tf_op jit(solution)/shard_map/ppermute | solution.py:28
  35.2 5.3 %collective-permute-start.6 = (f32[34,1,256]{2,1,0:T(1,128)S(1)}, f32[34,1,256]{2,1,0:T(1,128)S(1)}, u32[]{:S(2)}, u32[]{:S(2)}) collective-permute-start(f32[34,1,256]{2,1,0:T(1,128)S(1)} %get-tuple-element.51), channel_id=1, source_target_pairs={{0,1},{1,2},{2,3},{3,4},{4,5},{5,6},{6,7},{7,8},{8,9},{9,10},{10,1... | collective-permute-start | bytes 104456 | tf_op jit(solution)/shard_map/ppermute | solution.py:25
  37.1 6.8 %collective-permute-start.7 = (f32[34,1,256]{2,1,0:T(1,128)S(1)}, f32[34,1,256]{2,1,0:T(1,128)S(1)}, u32[]{:S(2)}, u32[]{:S(2)}) collective-permute-start(f32[34,1,256]{2,1,0:T(1,128)S(1)} %get-tuple-element.52), channel_id=1, source_target_pairs={{1,0},{2,1},{3,2},{4,3},{5,4},{6,5},{7,6},{8,7},{9,8},{10,9},{11,1... | collective-permute-start | bytes 104456 | tf_op jit(solution)/shard_map/ppermute | solution.py:28
  55.9 5.3 %collective-permute-start.10 = (f32[34,1,256]{2,1,0:T(1,128)S(1)}, f32[34,1,256]{2,1,0:T(1,128)S(1)}, u32[]{:S(2)}, u32[]{:S(2)}) collective-permute-start(f32[34,1,256]{2,1,0:T(1,128)S(1)} %get-tuple-element.49), channel_id=1, source_target_pairs={{0,1},{1,2},{2,3},{3,4},{4,5},{5,6},{6,7},{7,8},{8,9},{9,10},{10,1... | collective-permute-start | bytes 104456 | tf_op jit(solution)/shard_map/ppermute | solution.py:25
  57.8 6.8 %collective-permute-start.11 = (f32[34,1,256]{2,1,0:T(1,128)S(1)}, f32[34,1,256]{2,1,0:T(1,128)S(1)}, u32[]{:S(2)}, u32[]{:S(2)}) collective-permute-start(f32[34,1,256]{2,1,0:T(1,128)S(1)} %get-tuple-element.50), channel_id=1, source_target_pairs={{1,0},{2,1},{3,2},{4,3},{5,4},{6,5},{7,6},{8,7},{9,8},{10,9},{11,1... | collective-permute-start | bytes 104456 | tf_op jit(solution)/shard_map/ppermute | solution.py:28
  76.7 5.3 %collective-permute-start.14 = (f32[34,1,256]{2,1,0:T(1,128)S(1)}, f32[34,1,256]{2,1,0:T(1,128)S(1)}, u32[]{:S(2)}, u32[]{:S(2)}) collective-permute-start(f32[34,1,256]{2,1,0:T(1,128)S(1)} %get-tuple-element.47), channel_id=1, source_target_pairs={{0,1},{1,2},{2,3},{3,4},{4,5},{5,6},{6,7},{7,8},{8,9},{9,10},{10,1... | collective-permute-start | bytes 104456 | tf_op jit(solution)/shard_map/ppermute | solution.py:25
  78.6 6.8 %collective-permute-start.15 = (f32[34,1,256]{2,1,0:T(1,128)S(1)}, f32[34,1,256]{2,1,0:T(1,128)S(1)}, u32[]{:S(2)}, u32[]{:S(2)}) collective-permute-start(f32[34,1,256]{2,1,0:T(1,128)S(1)} %get-tuple-element.48), channel_id=1, source_target_pairs={{1,0},{2,1},{3,2},{4,3},{5,4},{6,5},{7,6},{8,7},{9,8},{10,9},{11,1... | collective-permute-start | bytes 104456 | tf_op jit(solution)/shard_map/ppermute | solution.py:28
  98.8 5.5 %collective-permute-start.18 = (f32[34,1,256]{2,1,0:T(1,128)S(1)}, f32[34,1,256]{2,1,0:T(1,128)S(1)}, u32[]{:S(2)}, u32[]{:S(2)}) collective-permute-start(f32[34,1,256]{2,1,0:T(1,128)S(1)} %get-tuple-element.45), channel_id=1, source_target_pairs={{0,1},{1,2},{2,3},{3,4},{4,5},{5,6},{6,7},{7,8},{8,9},{9,10},{10,1... | collective-permute-start | bytes 104456 | tf_op jit(solution)/shard_map/ppermute | solution.py:25
  100.7 6.8 %collective-permute-start.19 = (f32[34,1,256]{2,1,0:T(1,128)S(1)}, f32[34,1,256]{2,1,0:T(1,128)S(1)}, u32[]{:S(2)}, u32[]{:S(2)}) collective-permute-start(f32[34,1,256]{2,1,0:T(1,128)S(1)} %get-tuple-element.46), channel_id=1, source_target_pairs={{1,0},{2,1},{3,2},{4,3},{5,4},{6,5},{7,6},{8,7},{9,8},{10,9},{11,1... | collective-permute-start | bytes 104456 | tf_op jit(solution)/shard_map/ppermute | solution.py:28
  119.5 5.3 %collective-permute-start.22 = (f32[34,1,256]{2,1,0:T(1,128)S(1)}, f32[34,1,256]{2,1,0:T(1,128)S(1)}, u32[]{:S(2)}, u32[]{:S(2)}) collective-permute-start(f32[34,1,256]{2,1,0:T(1,128)S(1)} %get-tuple-element.43), channel_id=1, source_target_pairs={{0,1},{1,2},{2,3},{3,4},{4,5},{5,6},{6,7},{7,8},{8,9},{9,10},{10,1... | collective-permute-start | bytes 104456 | tf_op jit(solution)/shard_map/ppermute | solution.py:25
  121.5 6.8 %collective-permute-start.23 = (f32[34,1,256]{2,1,0:T(1,128)S(1)}, f32[34,1,256]{2,1,0:T(1,128)S(1)}, u32[]{:S(2)}, u32[]{:S(2)}) collective-permute-start(f32[34,1,256]{2,1,0:T(1,128)S(1)} %get-tuple-element.44), channel_id=1, source_target_pairs={{1,0},{2,1},{3,2},{4,3},{5,4},{6,5},{7,6},{8,7},{9,8},{10,9},{11,1... | collective-permute-start | bytes 104456 | tf_op jit(solution)/shard_map/ppermute | solution.py:28
  140.4 43.0 %collective-permute-start.26 = (f32[34,1,256]{2,1,0:T(1,128)S(1)}, f32[34,1,256]{2,1,0:T(1,128)S(1)}, u32[]{:S(2)}, u32[]{:S(2)}) collective-permute-start(f32[34,1,256]{2,1,0:T(1,128)S(1)} %get-tuple-element.41), channel_id=1, source_target_pairs={{0,1},{1,2},{2,3},{3,4},{4,5},{5,6},{6,7},{7,8},{8,9},{9,10},{10,1... | collective-permute-start | bytes 104456 | tf_op jit(solution)/shard_map/ppermute | solution.py:25
  142.3 41.1 %collective-permute-start.27 = (f32[34,1,256]{2,1,0:T(1,128)S(1)}, f32[34,1,256]{2,1,0:T(1,128)S(1)}, u32[]{:S(2)}, u32[]{:S(2)}) collective-permute-start(f32[34,1,256]{2,1,0:T(1,128)S(1)} %get-tuple-element.42), channel_id=1, source_target_pairs={{1,0},{2,1},{3,2},{4,3},{5,4},{6,5},{7,6},{8,7},{9,8},{10,9},{11,1... | collective-permute-start | bytes 104456 | tf_op jit(solution)/shard_map/ppermute | solution.py:28
  192.3 12.5 %collective-permute-start.28 = (f32[1,32,256]{2,1,0:T(8,128)S(1)}, f32[1,32,256]{2,1,0:T(8,128)S(1)}, u32[]{:S(2)}, u32[]{:S(2)}) collective-permute-start(f32[1,32,256]{2,1,0:T(8,128)S(1)} %get-tuple-element.59), channel_id=1, source_target_pairs={{0,16},{16,32},{32,48},{48,64},{64,80},{80,96},{96,112},{1,17},{17... | collective-permute-start | bytes 98312 | tf_op jit(solution)/shard_map/ppermute | solution.py:25
  208.2 7.4 %collective-permute-start.30 = (f32[34,1,256]{2,1,0:T(1,128)S(1)}, f32[34,1,256]{2,1,0:T(1,128)S(1)}, u32[]{:S(2)}, u32[]{:S(2)}) collective-permute-start(f32[34,1,256]{2,1,0:T(1,128)S(1)} %get-tuple-element.39), channel_id=1, source_target_pairs={{0,1},{1,2},{2,3},{3,4},{4,5},{5,6},{6,7},{7,8},{8,9},{9,10},{10,1... | collective-permute-start | bytes 104456 | tf_op jit(solution)/shard_map/ppermute | solution.py:25
  213.7 6.8 %collective-permute-start.31 = (f32[34,1,256]{2,1,0:T(1,128)S(1)}, f32[34,1,256]{2,1,0:T(1,128)S(1)}, u32[]{:S(2)}, u32[]{:S(2)}) collective-permute-start(f32[34,1,256]{2,1,0:T(1,128)S(1)} %get-tuple-element.40), channel_id=1, source_target_pairs={{1,0},{2,1},{3,2},{4,3},{5,4},{6,5},{7,6},{8,7},{9,8},{10,9},{11,1... | collective-permute-start | bytes 104456 | tf_op jit(solution)/shard_map/ppermute | solution.py:28
  224.9 5.5 %collective-permute-start.32 = (f32[1,32,256]{2,1,0:T(8,128)S(1)}, f32[1,32,256]{2,1,0:T(8,128)S(1)}, u32[]{:S(2)}, u32[]{:S(2)}) collective-permute-start(f32[1,32,256]{2,1,0:T(8,128)S(1)} %get-tuple-element.57), channel_id=1, source_target_pairs={{0,16},{16,32},{32,48},{48,64},{64,80},{80,96},{96,112},{1,17},{17... | collective-permute-start | bytes 98312 | tf_op jit(solution)/shard_map/ppermute | solution.py:25
  233.8 46.7 %collective-permute-start.34 = (f32[34,1,256]{2,1,0:T(1,128)S(1)}, f32[34,1,256]{2,1,0:T(1,128)S(1)}, u32[]{:S(2)}, u32[]{:S(2)}) collective-permute-start(f32[34,1,256]{2,1,0:T(1,128)S(1)} %get-tuple-element.37), channel_id=1, source_target_pairs={{0,1},{1,2},{2,3},{3,4},{4,5},{5,6},{6,7},{7,8},{8,9},{9,10},{10,1... | collective-permute-start | bytes 104456 | tf_op jit(solution)/shard_map/ppermute | solution.py:25
  235.7 44.8 %collective-permute-start.35 = (f32[34,1,256]{2,1,0:T(1,128)S(1)}, f32[34,1,256]{2,1,0:T(1,128)S(1)}, u32[]{:S(2)}, u32[]{:S(2)}) collective-permute-start(f32[34,1,256]{2,1,0:T(1,128)S(1)} %get-tuple-element.38), channel_id=1, source_target_pairs={{1,0},{2,1},{3,2},{4,3},{5,4},{6,5},{7,6},{8,7},{9,8},{10,9},{11,1... | collective-permute-start | bytes 104456 | tf_op jit(solution)/shard_map/ppermute | solution.py:28
  290.3 13.1 %collective-permute-start.36 = (f32[1,32,256]{2,1,0:T(8,128)S(1)}, f32[1,32,256]{2,1,0:T(8,128)S(1)}, u32[]{:S(2)}, u32[]{:S(2)}) collective-permute-start(f32[1,32,256]{2,1,0:T(8,128)S(1)} %get-tuple-element.55), channel_id=1, source_target_pairs={{0,16},{16,32},{32,48},{48,64},{64,80},{80,96},{96,112},{1,17},{17... | collective-permute-start | bytes 98312 | tf_op jit(solution)/shard_map/ppermute | solution.py:25
  306.4 9.5 %collective-permute-start.38 = (f32[34,1,256]{2,1,0:T(1,128)S(1)}, f32[34,1,256]{2,1,0:T(1,128)S(1)}, u32[]{:S(2)}, u32[]{:S(2)}) collective-permute-start(f32[34,1,256]{2,1,0:T(1,128)S(1)} %get-tuple-element.35), channel_id=1, source_target_pairs={{0,1},{1,2},{2,3},{3,4},{4,5},{5,6},{6,7},{7,8},{8,9},{9,10},{10,1... | collective-permute-start | bytes 104456 | tf_op jit(solution)/shard_map/ppermute | solution.py:25
  312.0 6.8 %collective-permute-start.39 = (f32[34,1,256]{2,1,0:T(1,128)S(1)}, f32[34,1,256]{2,1,0:T(1,128)S(1)}, u32[]{:S(2)}, u32[]{:S(2)}) collective-permute-start(f32[34,1,256]{2,1,0:T(1,128)S(1)} %get-tuple-element.36), channel_id=1, source_target_pairs={{1,0},{2,1},{3,2},{4,3},{5,4},{6,5},{7,6},{8,7},{9,8},{10,9},{11,1... | collective-permute-start | bytes 104456 | tf_op jit(solution)/shard_map/ppermute | solution.py:28
  (42 other events, 781.9 us)
